TPU v7x, 1024 devices: a whole 4x4x32 slice. The times are simulated.
1024 devices in a mesh: pipe: 4 (over y), expert: 64 (over z, core), tensor: 4 (over x).
Axes of the slice: x: 4, y: 4, z: 32, core: 2. Of those that a mesh axis runs over, the one named last changes fastest.
Arguments:
- sent_grad: bfloat16 [4, 8192, 3584], P('pipe', 'expert', 'tensor'), may hold values from -4 to 4
- head_grad: bfloat16 [8192, 3584], P('expert', 'tensor'), may hold values from -4 to 4
- probs: bfloat16 [4, 8192, 8], P('pipe', 'expert'), may hold values from 0.049804688 to 1
- expert_ids: int32 [4, 8192, 8], P('pipe', 'expert'), may hold values from 0 to 63, as said below
- hidden_act: bfloat16 [4, 64, 1088, 1024], P('pipe', 'expert', None, 'tensor'), may hold values from -0.1875 to 0.1875
Outputs:
- w_down_grad: bfloat16 [4, 64, 1024, 3584], P('pipe', 'expert', 'tensor')
Inputs may be any that keep to these rules, and one draw needn't show every extreme that they name: `expert_ids`: each token names 8 different experts. In each section and each block of 128 tokens one expert is named by exactly 17 pairs, one by 17 - 2 pairs, and every other expert by 17 - 1 pairs.
All inputs are finite; a program needn't handle non-finite values.
Results may differ from a plain program's by a relative error of at most 0.0049.
Values may be sent and summed in bfloat16 or wider, within the bound.
A program may use at most 32 MiB of HBM per device.

v0:
```python
import jax
import jax.numpy as jnp
from jax import lax
from jax.sharding import PartitionSpec as P

EXPERTS = 64
TOPK = 8
TOK = 128
MOST = 17


def passed_along(array, axis, by):
    peers = lax.axis_size(axis)
    pairs = [(i, i + by) for i in range(peers) if 0 <= i + by < peers]
    return lax.ppermute(array, axis, pairs)


def slot_ranks(pair_ids):
    onehot = (pair_ids[:, :, None] == jnp.arange(EXPERTS, dtype=jnp.int32)[None, None, :]).astype(
        jnp.int32
    )
    before = jnp.cumsum(onehot, axis=1) - onehot
    return jnp.sum(before * onehot, axis=2)


def place_rows(targets, capacity, source_rows, gate_values):
    pair_count = targets.shape[0]
    owner_pair = (
        jnp.full((capacity,), pair_count, jnp.int32)
        .at[targets]
        .set(jnp.arange(pair_count, dtype=jnp.int32), mode="drop")
    )
    filled = owner_pair < pair_count
    safe_pair = jnp.minimum(owner_pair, pair_count - 1)
    placed = jnp.where(
        filled[:, None], source_rows[safe_pair // TOPK], jnp.zeros((), source_rows.dtype)
    )
    placed_gate = jnp.where(
        filled, gate_values.reshape(-1)[safe_pair], jnp.zeros((), gate_values.dtype)
    )
    return (placed, placed_gate)


def local(sent_grad, head_grad, probs, expert_ids, hidden_act):
    shifted = passed_along(sent_grad, "pipe", -1)
    is_last = lax.axis_index("pipe") == lax.axis_size("pipe") - 1
    incoming = jnp.where(is_last, head_grad, shifted[0])
    feat_dev = incoming.shape[1]
    local_ids = expert_ids[0].reshape(1, TOK * TOPK)
    local_targets = (local_ids * MOST + slot_ranks(local_ids)).reshape(-1)
    send_rows, send_gate = place_rows(local_targets, EXPERTS * MOST, incoming, probs[0])
    recv_rows, recv_gate = (
        lax.all_to_all(
            send_rows.reshape(EXPERTS, MOST, feat_dev),
            "expert",
            split_axis=0,
            concat_axis=1,
            tiled=True,
        ),
        lax.all_to_all(
            send_gate.reshape(EXPERTS, MOST), "expert", split_axis=0, concat_axis=1, tiled=True
        ),
    )
    gate_wide = recv_gate.astype(jnp.float32)[:, :, None]
    full_rows = lax.all_gather(recv_rows, "tensor", axis=2, tiled=True)
    weighted = (full_rows.astype(jnp.float32) * gate_wide).astype(jnp.bfloat16)
    weight_grad = jnp.einsum(
        "esh,esd->ehd", hidden_act[0], weighted, preferred_element_type=jnp.float32
    ).astype(jnp.bfloat16)
    return weight_grad[None]


def solution(mesh):
    in_specs = (
        P("pipe", "expert", "tensor"),
        P("expert", "tensor"),
        P("pipe", "expert", None),
        P("pipe", "expert", None),
        P("pipe", "expert", None, "tensor"),
    )
    out_specs = P("pipe", "expert", "tensor", None)
    return jax.shard_map(local, mesh=mesh, in_specs=in_specs, out_specs=out_specs, check_vma=False)
```

profile of v0, /device:TPU:1, one launch (start us, length us, event | category | flops | bytes accessed | tf_op | source)
XLA Modules:
  0.0 431.4 jit_solution(16469606993573941667)
XLA Ops:
  6.5 0.0 copy-start
  6.5 0.0 copy-start.2
  6.5 0.0 all-gather.2.cloned.1.call-start
  6.5 1.4 collective-permute-start
  8.0 0.8 copy.14
  8.8 0.1 eq.30
  8.9 18.0 %reduce-window.6 = s32[1,64,8,128]{3,2,1,0:T(8,128)S(1)} reduce-window(s32[1,64,8,128]{3,2,1,0:T(8,128)S(1)} %bitcast.31, s32[]{:T(128)} %constant.16.clone.1), window={size=1x1x1x128 pad=0_0x0_0x0_0x127_0}, to_apply=%region_0.1 | reduce-window | flops 8323072 | bytes 524292 | tf_op jit(solution)/shard_map/reduce-window
  26.9 0.1 slice.12
  27.1 0.7 broadcast_multiply_fusion
  27.8 0.1 copy.15
  28.0 0.1 copy.16
  28.1 0.1 broadcast.90
  28.2 0.0 copy-start.1
  28.3 0.1 copy.13
  28.4 0.1 mul.32
  28.5 0.1 fusion.12
  28.6 4.3 %scatter_custom_fusion = s32[1088]{0:T(1024)S(1)} fusion(s32[1024]{0:T(1024)S(1)} %bitcast.34, s32[1024]{0:T(1024)S(1)} %iota.15, s32[]{:T(128)} %constant.13.clone.1), kind=kCustom, calls=%fused_computation.32 | custom fusion | bytes 4356 | tf_op jit(solution)/shard_map/scatter | solution.py:31
  33.0 0.0 copy-done.2
  33.0 0.1 copy.17
  33.1 0.1 reshape_squeeze.4
  33.2 6.9 %gather_fusion.1 = bf16[1088]{0:T(1024)(128)(2,1)S(1)} fusion(bf16[1024]{0:T(1024)(128)(2,1)S(1)} %reshape_squeeze.4, s32[2048]{0:T(1024)S(1)} %pad_clamp_fusion), kind=kCustom, calls=%fused_computation.1 | custom fusion | bytes 8704 | tf_op jit(solution)/shard_map/gather | solution.py:39
  40.1 0.1 broadcast_in_dim.31
  40.3 0.0 collective-permute-done
  40.3 0.0 copy-done.1
  40.4 4.8 %gather_fusion = bf16[1088,896]{1,0:T(8,128)(2,1)} fusion(bf16[128,896]{1,0:T(8,128)(2,1)S(1)} %bitcast_select_fusion, s32[2048]{0:T(1024)S(1)} %pad_clamp_fusion.1), kind=kCustom, calls=%fused_computation | custom fusion | bytes 3903744 | tf_op jit(solution)/shard_map/gather | solution.py:36
  45.2 2.6 gather.9
  47.9 0.4 broadcast_select_fusion
  48.3 285.6 %all_to_all.26 = bf16[64,17,896]{2,1,0:T(8,128)(2,1)S(1)} all-to-all(bf16[64,17,896]{2,1,0:T(8,128)(2,1)S(1)} %broadcast_select_fusion), channel_id=1, replica_groups=mesh['pipe'=4,'expert'=64,'tensor'=4] {'expert'}, dimensions={0} | all-to-all | bytes 3899392 | tf_op jit(solution)/shard_map/all_to_all | solution.py:53
  333.9 2.2 all_to_all.20
  336.0 0.0 all-gather.2.cloned.1.call-update
  336.1 0.2 all_to_all.23
  336.2 27.1 %all_to_all.27 = bf16[64,1,17]{2,1,0:T(2,128)(2,1)S(1)} all-to-all(bf16[64,1,17]{2,1,0:T(2,128)(2,1)S(1)} %all_to_all.23), channel_id=1, replica_groups=mesh['pipe'=4,'expert'=64,'tensor'=4] {'expert'}, dimensions={0} | all-to-all | bytes 4352 | tf_op jit(solution)/shard_map/all_to_all | solution.py:60
  363.3 0.1 convert_reduce_fusion
  363.4 0.1 reshape.200
  363.6 52.1 %all-gather.2.cloned.1.call-done = bf16[1,1088,3584]{2,1,0:T(8,128)(2,1)} async-done(((bf16[1,1088,896]{2,1,0:T(8,128)(2,1)}), bf16[1,1088,3584]{2,1,0:T(8,128)(2,1)}) %all-gather.2.cloned.1.call-update) | async-done | bytes 7798800 | tf_op jit(solution)/shard_map/all_gather | solution.py:65
  415.7 0.0 copy-done
  415.7 6.2 %fusion.7 = bf16[1,1,256,3584]{2,3,1,0:T(8,128)(2,1)S(1)} fusion(bf16[1,1088,3584]{2,1,0:T(8,128)(2,1)} %all-gather.2.cloned.1.call-done, f32[1088]{0:T(1024)S(1)} %reshape.200, bf16[1,1,1088,256]{3,2,1,0:T(8,128)(2,1)S(1)} %copy-done), kind=kOutput, calls=%fused_computation.8 | convolution fusion | flops 2009104384 | bytes 10195200 | tf_op jit(solution)/shard_map/esh,esd->ehd/dot_general | solution.py:67
  422.0 2.6 copy.19
  (13 shorter events, 0.3 us)
Async XLA Ops:
  6.5 409.2 %copy-start = (bf16[1,1,1088,256]{3,2,1,0:T(8,128)(2,1)S(1)}, bf16[1,1,1088,256]{3,2,1,0:T(8,128)(2,1)}, u32[]{:S(2)}) copy-start(bf16[1,1,1088,256]{3,2,1,0:T(8,128)(2,1)} %param.9) | copy-start | bytes 1671172
  6.5 26.4 %copy-start.2 = (bf16[1,128,8]{1,2,0:T(8,128)(2,1)S(1)}, bf16[1,128,8]{1,2,0:T(8,128)(2,1)}, u32[]{:S(2)}) copy-start(bf16[1,128,8]{1,2,0:T(8,128)(2,1)} %param.7) | copy-start | bytes 6148
  6.5 409.2 %all-gather.2.cloned.1.call-start = ((), (), s32[]{:S(2)}) async-start(), calls=%async_computation.2 | async-start | bytes 9748480 | tf_op jit(solution)/shard_map/all_gather | solution.py:65
  6.5 33.8 %collective-permute-start = (bf16[1,128,896]{2,1,0:T(8,128)(2,1)}, bf16[1,128,896]{2,1,0:T(8,128)(2,1)S(1)}, u32[]{:S(2)}, u32[]{:S(2)}) collective-permute-start(bf16[1,128,896]{2,1,0:T(8,128)(2,1)} %param.5), channel_id=1, source_target_pairs={{256,0},{512,256},{768,512},{257,1},{513,257},{769,513},{258,2},{5... | collective-permute-start | bytes 688136 | tf_op jit(solution)/shard_map/ppermute | solution.py:15
  28.2 12.1 %copy-start.1 = (bf16[128,896]{1,0:T(8,128)(2,1)S(1)}, bf16[128,896]{1,0:T(8,128)(2,1)}, u32[]{:S(2)}) copy-start(bf16[128,896]{1,0:T(8,128)(2,1)} %param.6) | copy-start | bytes 688132
Sparse Core Ops, SparseCore 0:
  336.2 79.4 all-gather.1
where the time goes:
time: 432 us; the launch traced here: 431 us
  blocking collectives  313 us (72%)
  waiting for transfers between devices  52.2 us (12%)
  local copies, waits for them, and re-layouts  25.9 us (6%)
  other arithmetic  19.4 us (4%)
  between operations  13.6 us (3%)
  matrix products  6.23 us (1%)
    all_to_all x1, blocking collectives, local(): lax.all_to_all(send_rows.reshape(EXPERTS, MOST, feat_dev), 'expert', spli...  286 us
    all_gather x1, waiting for transfers between devices, local(): full_rows = lax.all_gather(recv_rows, 'tensor', axis=2, tiled=True)  52.1 us
    all_to_all x1, blocking collectives, local(): lax.all_to_all(send_gate.reshape(EXPERTS, MOST), 'expert', split_axis=0,...  27.1 us
    another operation x2, other arithmetic  18 us
  transfers between devices with their start and end apart: 2, of which 1 were waited for; matrix products, arithmetic and copies ran while one was open for 8% of the time, Pallas kernels for 0%

commit v1 on v0

v1 whole, which is shorter than its diff:
```python
import jax
import jax.numpy as jnp
from jax import lax
from jax.sharding import PartitionSpec as P

EXPERTS = 64
TOPK = 8
TOK = 128
MOST = 17


def local(sent_grad, head_grad, probs, expert_ids, hidden_act):
    pipes = lax.axis_size("pipe")
    pairs = [(i, i - 1) for i in range(1, pipes)]
    shifted = lax.ppermute(sent_grad, "pipe", pairs)
    is_last = lax.axis_index("pipe") == pipes - 1
    incoming = jnp.where(is_last, head_grad, shifted[0])
    meta = jnp.concatenate([expert_ids[0].T.astype(jnp.bfloat16), probs[0].T], axis=0)
    metas = lax.all_gather(meta, "expert", axis=0)
    tokens = lax.all_gather(incoming, "expert", axis=0)
    me = lax.axis_index("expert").astype(jnp.bfloat16)
    hit = metas[:, :TOPK, :] == me
    gate = jnp.sum(jnp.where(hit, metas[:, TOPK:, :], 0).astype(jnp.float32), axis=1)
    routed = jnp.any(hit, axis=1)
    upper = (jnp.arange(TOK)[:, None] < jnp.arange(TOK)[None, :]).astype(jnp.bfloat16)
    rank = jnp.dot(routed.astype(jnp.bfloat16), upper, preferred_element_type=jnp.float32)
    slot = jnp.where(routed, rank, -1.0).astype(jnp.int32)
    pick = jnp.where(
        slot[:, None, :] == jnp.arange(MOST, dtype=jnp.int32)[None, :, None], gate[:, None, :], 0.0
    ).astype(jnp.bfloat16)
    weighted = jnp.einsum(
        "brn,bnd->brd", pick, tokens, preferred_element_type=jnp.float32
    ).astype(jnp.bfloat16)
    rows = weighted.reshape(EXPERTS * MOST, -1)
    full = lax.all_gather(rows, "tensor", axis=1, tiled=True)
    grad = jnp.einsum("sh,sd->hd", hidden_act[0, 0], full, preferred_element_type=jnp.float32)
    return grad.astype(jnp.bfloat16)[None, None]


def solution(mesh):
    in_specs = (
        P("pipe", "expert", "tensor"),
        P("expert", "tensor"),
        P("pipe", "expert", None),
        P("pipe", "expert", None),
        P("pipe", "expert", None, "tensor"),
    )
    out_specs = P("pipe", "expert", "tensor", None)
    return jax.shard_map(local, mesh=mesh, in_specs=in_specs, out_specs=out_specs, check_vma=False)
```

time: 432 us -> 290 us (0.67)
  blocking collectives: 313 us -> 72.6 us
  waiting for transfers between devices: 52.2 us -> 182 us
  local copies, waits for them, and re-layouts: 25.9 us -> 4.79 us
  other arithmetic: 19.4 us -> 2.3 us
  matrix products: 6.23 us -> 13.4 us
    all_to_all x2 -> x0, blocking collectives: 313 us -> none  [the longest x1 286 us: local(): lax.all_to_all(send_rows.reshape(EXPERTS, MOST, feat_dev), 'expert', spli...]
    all_gather x1 -> x2, waiting for transfers between devices: 52.1 us -> 175 us  [the longest x1 89.1 us: local(): tokens = lax.all_gather(incoming, 'expert', axis=0)]
    all_gather x0 -> x1, blocking collectives: none -> 72.6 us  [local(): metas = lax.all_gather(meta, 'expert', axis=0)]
    another operation x2 -> x0, other arithmetic: 18 us -> none
    gather x3 -> x0, local copies, waits for them, and re-layouts: 14.4 us -> none  [the longest x2 7.49 us: place_rows(): source_rows[safe_pair // TOPK]]
    dot_general x1 -> x3, matrix products: 6.23 us -> 13.4 us  [the longest x1 7.47 us: local(): jnp.einsum('brn,bnd->brd', pick, tokens, preferred_element_type=jnp.float32)]
    ppermute x1, waiting for transfers between devices: 0.01 us -> 6.34 us  [local(): shifted = lax.ppermute(sent_grad, 'pipe', pairs)]
  transfers between devices with their start and end apart: 2 -> 3, of which waited for: 1 -> 3; matrix products, arithmetic and copies ran while one was open for 8% -> 1% of each run, Pallas kernels for 0% -> 0%
where the time goes in v1:
time: 290 us
  waiting for transfers between devices  182 us (63%)
  blocking collectives  72.6 us (25%)
  matrix products  13.4 us (5%)
  between operations  13.4 us (5%)
  local copies, waits for them, and re-layouts  4.79 us (2%)
    all_gather x1, waiting for transfers between devices, local(): tokens = lax.all_gather(incoming, 'expert', axis=0)  89.1 us
    all_gather x1, waiting for transfers between devices, local(): full = lax.all_gather(rows, 'tensor', axis=1, tiled=True)  86.4 us
    all_gather x1, blocking collectives, local(): metas = lax.all_gather(meta, 'expert', axis=0)  72.6 us
    dot_general x1, matrix products, local(): jnp.einsum('brn,bnd->brd', pick, tokens, preferred_element_type=jnp.float32)  7.47 us
    ppermute x1, waiting for transfers between devices, local(): shifted = lax.ppermute(sent_grad, 'pipe', pairs)  6.34 us
    dot_general x1, matrix products, local(): jnp.einsum('sh,sd->hd', hidden_act[0, 0], full, preferred_element_type=jn...  5.82 us
  transfers between devices with their start and end apart: 3, of which 3 were waited for; matrix products, arithmetic and copies ran while one was open for 1% of the time, Pallas kernels for 0%

profile of v1, /device:TPU:1, one launch (start us, length us, event | category | flops | bytes accessed | tf_op | source)
XLA Modules:
  0.0 289.9 jit_solution(12072415379007970148)
XLA Ops:
  6.5 0.0 copy-start
  6.5 0.0 all-gather.7.cloned.1.call-start
  6.5 1.4 collective-permute-start
  8.0 6.3 %collective-permute-done = bf16[1,128,896]{2,1,0:T(8,128)(2,1)S(1)} collective-permute-done((bf16[1,128,896]{2,1,0:T(8,128)(2,1)}, bf16[1,128,896]{2,1,0:T(8,128)(2,1)S(1)}, u32[]{:S(2)}, u32[]{:S(2)}) %collective-permute-start) | collective-permute-done | bytes 229408 | tf_op jit(solution)/shard_map/ppermute | solution.py:15
  14.3 0.7 bitcast_select_fusion
  15.0 0.0 all-gather.7.cloned.1.call-update
  15.1 0.0 all-gather.5.cloned.1.call-start
  15.1 0.7 convert_bitcast_fusion
  15.8 0.7 pad_maximum_fusion
  16.5 72.6 %all-gather = bf16[1024,128]{1,0:T(8,128)(2,1)S(1)} all-gather(bf16[16,128]{1,0:T(8,128)(2,1)S(1)} %pad_maximum_fusion), channel_id=2, replica_groups=mesh['pipe'=4,'expert'=64,'tensor'=4] {'expert'}, dimensions={0}, use_global_device_ids=true | all-gather | bytes 266240 | tf_op jit(solution)/shard_map/all_gather | solution.py:19
  89.1 0.1 fusion.6
  89.2 0.1 convert_reduce_fusion
  89.3 0.1 fusion.1
  89.5 89.1 %all-gather.7.cloned.1.call-done = bf16[8192,896]{1,0:T(8,128)(2,1)} async-done(((bf16[128,896]{1,0:T(8,128)(2,1)}), bf16[8192,896]{1,0:T(8,128)(2,1)}) %all-gather.7.cloned.1.call-update) | async-done | bytes 14680080 | tf_op jit(solution)/shard_map/all_gather | solution.py:20
  178.6 7.5 %convolution_convert_fusion.1 = bf16[64,17,896]{2,1,0:T(8,128)(2,1)S(1)} fusion(bf16[64,128,896]{2,1,0:T(8,128)(2,1)} %bitcast.21, bf16[64,128]{1,0:T(8,128)(2,1)S(1)} %convert_reduce_fusion, s32[64,128]{1,0:T(8,128)S(1)} %fusion.1), kind=kOutput, calls=%fused_computation.2 | convolution fusion | flops 250814464 | bytes 16678912 | tf_op jit(solution)/shard_map/brn,bnd->brd/dot_general | solution.py:31
  186.1 2.2 reshape.6
  188.3 0.0 all-gather.5.cloned.1.call-update
  188.3 86.4 %all-gather.5.cloned.1.call-done = bf16[1088,3584]{1,0:T(8,128)(2,1)} async-done(((bf16[1088,896]{1,0:T(8,128)(2,1)}), bf16[1088,3584]{1,0:T(8,128)(2,1)}) %all-gather.5.cloned.1.call-update) | async-done | bytes 7798800 | tf_op jit(solution)/shard_map/all_gather | solution.py:35
  274.7 0.0 copy-done
  274.7 5.8 %fusion = bf16[1,1,256,3584]{2,3,1,0:T(8,128)(2,1)S(1)} fusion(bf16[1088,3584]{1,0:T(8,128)(2,1)} %all-gather.5.cloned.1.call-done, bf16[1,1,1088,256]{3,2,1,0:T(8,128)(2,1)S(1)} %copy-done), kind=kOutput, calls=%fused_computation.1 | convolution fusion | flops 1997406208 | bytes 10190848 | tf_op jit(solution)/shard_map/sh,sd->hd/dot_general | solution.py:36
  280.5 2.6 copy.7
Async XLA Ops:
  6.5 268.1 %copy-start = (bf16[1,1,1088,256]{3,2,1,0:T(8,128)(2,1)S(1)}, bf16[1,1,1088,256]{3,2,1,0:T(8,128)(2,1)}, u32[]{:S(2)}) copy-start(bf16[1,1,1088,256]{3,2,1,0:T(8,128)(2,1)} %param.9) | copy-start | bytes 1671172
  6.5 172.0 %all-gather.7.cloned.1.call-start = ((), (), s32[]{:S(2)}) async-start(), calls=%async_computation.1 | async-start | bytes 14909440 | tf_op jit(solution)/shard_map/all_gather | solution.py:20
  6.5 7.8 %collective-permute-start = (bf16[1,128,896]{2,1,0:T(8,128)(2,1)}, bf16[1,128,896]{2,1,0:T(8,128)(2,1)S(1)}, u32[]{:S(2)}, u32[]{:S(2)}) collective-permute-start(bf16[1,128,896]{2,1,0:T(8,128)(2,1)} %param.5), channel_id=1, source_target_pairs={{256,0},{512,256},{768,512},{257,1},{513,257},{769,513},{258,2},{5... | collective-permute-start | bytes 688136 | tf_op jit(solution)/shard_map/ppermute | solution.py:15
  15.1 259.6 %all-gather.5.cloned.1.call-start = ((), (), s32[]{:S(2)}) async-start(), calls=%async_computation | async-start | bytes 9748480 | tf_op jit(solution)/shard_map/all_gather | solution.py:35
Sparse Core Ops, SparseCore 0:
  15.2 163.3 all-gather.6
  188.4 86.2 all-gather.4

commit v2 on v1

v2 whole, which is shorter than its diff:
```python
import functools

import jax
import jax.numpy as jnp
from jax import lax
from jax.experimental import pallas as pl
from jax.experimental.pallas import tpu as pltpu
from jax.sharding import PartitionSpec as P

TOPK = 8
MOST = 17
CHUNKS = 4
MESH = pl.DeviceIdType.MESH


def kernel(
    pipes,
    chips,
    sides,
    meta_ref,
    hidden_ref,
    sent_ref,
    head_ref,
    out_ref,
    tokens,
    metas,
    pick,
    hidden,
    rows,
    acc,
    out_buf,
    own_sem,
    own_send,
    next_send,
    next_recv,
    prev_send,
    prev_recv,
    twin_send,
    twin_recv,
    side_send,
    side_recv,
    out_sem,
):
    tok, feat = sent_ref.shape
    piece = tok // CHUNKS
    half = chips // 2
    units = chips // 4
    block = 8 * tok
    unit_slots = 8 * MOST
    pad_slots = rows.shape[1] // units
    first = (pad_slots // 32) * 16 + (16 if pad_slots % 32 else 0)
    hid = hidden_ref.shape[1]

    me = lax.axis_index("expert")
    pipe = lax.axis_index("pipe")
    side = lax.axis_index("tensor")
    z = me // 2
    core = me % 2
    experts = 2 * chips
    to_next = {"expert": lax.rem(me + 2, experts)}
    to_prev = {"expert": lax.rem(me + experts - 2, experts)}
    to_twin = {"expert": me + 1 - 2 * core}
    to_right = {"tensor": lax.rem(side + 1, sides)}
    to_left = {"tensor": lax.rem(side + sides - 1, sides)}
    to_lower = {"pipe": lax.rem(pipe + pipes - 1, pipes)}
    to_upper = {"pipe": lax.rem(pipe + 1, pipes)}

    def place_up(d):
        return 4 * (d // 2) + d % 2

    def place_down(d):
        return 4 * ((d - 1) // 2) + 2 + (d - 1) % 2

    def part(place, parity, index):
        start = pl.multiple_of((place * 2 + parity) * tok + index * piece, piece)
        return tokens.at[pl.ds(start, piece), :]

    def whole(place, parity):
        return tokens.at[pl.ds(pl.multiple_of((place * 2 + parity) * tok, tok), tok), :]

    def remote(src, dst, send, recv, device):
        return pltpu.make_async_remote_copy(
            src_ref=src,
            dst_ref=dst,
            send_sem=send,
            recv_sem=recv,
            device_id=device,
            device_id_type=MESH,
        )

    def own_local(index):
        span = pl.ds(index * piece, piece)
        return pltpu.make_async_copy(
            head_ref.at[span, :], part(0, core, index), own_sem.at[index]
        )

    def own_remote(index):
        span = pl.ds(index * piece, piece)
        return remote(
            sent_ref.at[span, :],
            part(0, core, index),
            own_send.at[index],
            own_sem.at[index],
            to_lower,
        )

    def ring(send, recv, device, src, dst, step, index):
        if index < CHUNKS:
            a, b = part(src, core, index), part(dst, core, index)
        else:
            a, b = metas.at[src * 2 + core], metas.at[dst * 2 + core]
        return remote(a, b, send.at[step % 2, index], recv.at[step + 1, index], device)

    def next_copy(step, index):
        src = place_down(step) if not isinstance(step, int) or step > 0 else 0
        return ring(next_send, next_recv, to_next, src, place_down(step + 1), step, index)

    def prev_copy(step, index):
        far = place_up(step + 1)
        dst = jnp.where(step + 1 == half, place_down(half), far)
        return ring(prev_send, prev_recv, to_prev, place_up(step), dst, step, index)

    def twin_copies(place, parity, way, slot):
        return (
            remote(
                whole(place, parity),
                whole(place, parity),
                twin_send.at[way, slot, 0],
                twin_recv.at[place, 0],
                to_twin,
            ),
            remote(
                metas.at[place * 2 + parity],
                metas.at[place * 2 + parity],
                twin_send.at[way, slot, 1],
                twin_recv.at[place, 1],
                to_twin,
            ),
        )

    def row_span(unit, start, size):
        return pl.ds(pl.multiple_of(unit * pad_slots + start, 16), size)

    def side_copy(unit, which):
        a = row_span(unit, 0, first)
        b = row_span(unit, first, pad_slots - first)
        src, dst, span, device = (
            (0, 2, a, to_right),
            (0, 2, b, to_right),
            (0, 1, b, to_left),
            (0, 1, a, to_left),
            (2, 3, a, to_right),
            (1, 3, b, to_left),
        )[which]
        return remote(
            rows.at[src, span, :],
            rows.at[dst, span, :],
            side_send.at[unit, which],
            side_recv.at[unit, which],
            device,
        )

    own_meta = pltpu.make_async_copy(meta_ref, metas.at[core], out_sem.at[0])
    own_meta.start()

    @pl.when(pipe == pipes - 1)
    def _():
        for index in range(CHUNKS):
            own_local(index).start()

    barrier = pltpu.get_barrier_semaphore()
    for device in (to_next, to_prev, to_twin, to_right, to_left, to_lower, to_upper):
        pl.semaphore_signal(barrier, inc=1, device_id=device, device_id_type=MESH)
    pl.semaphore_wait(barrier, 7)

    @pl.when(pipe > 0)
    def _():
        for index in range(CHUNKS):
            own_remote(index).start()

    own_meta.wait()
    next_copy(0, CHUNKS).start()
    prev_copy(0, CHUNKS).start()
    for index in range(CHUNKS):

        @pl.when(pipe == pipes - 1)
        def _():
            own_local(index).wait()

        @pl.when(pipe < pipes - 1)
        def _():
            own_remote(index).wait_recv()

        next_copy(0, index).start()
        prev_copy(0, index).start()
    for copy in twin_copies(0, core, 0, 0):
        copy.start()

    slot_iota = lax.broadcasted_iota(jnp.int32, (pad_slots, tok), 0).astype(jnp.float32)
    before = (
        lax.broadcasted_iota(jnp.int32, (tok, tok), 0)
        < lax.broadcasted_iota(jnp.int32, (tok, tok), 1)
    ).astype(jnp.float32)
    mine = me.astype(jnp.float32)

    def unit_places(unit):
        return [4 * unit + q for q in range(4)]

    def prepare(unit):
        for place in unit_places(unit):
            for copy in twin_copies(place, 1 - core, 0, 0):
                copy.wait_recv()
        gates, hits = [], []
        for b in range(8):
            meta = metas[unit * 8 + b].astype(jnp.float32)
            hit = meta[:TOPK] == mine
            gates.append(jnp.sum(jnp.where(hit, meta[TOPK:], 0.0), axis=0, keepdims=True))
            hits.append(jnp.sum(jnp.where(hit, 1.0, 0.0), axis=0, keepdims=True))
        routed = jnp.concatenate(hits, axis=0)
        rank = jnp.dot(routed, before, preferred_element_type=jnp.float32)
        for b in range(8):
            slot = jnp.where(routed[b : b + 1] > 0.5, rank[b : b + 1] + b * MOST, -1.0)
            pick[:, b * tok : (b + 1) * tok] = jnp.where(
                slot_iota == slot, gates[b], 0.0
            ).astype(jnp.bfloat16)
        total = hidden_ref.shape[0]
        i = lax.broadcasted_iota(jnp.int32, (pad_slots, total), 0)
        width = 2 * MOST
        offsets = (2 * unit, 2 * unit + 1, chips - 2 * unit - 1, chips - 2 * unit - 2)
        target = jnp.full((pad_slots, total), -1, jnp.int32)
        for q in range(4):
            chip = lax.rem(z + offsets[q], chips)
            inside = (i >= q * width) & (i < (q + 1) * width)
            target = jnp.where(inside, i + (chip - q) * width, target)
        order = (lax.broadcasted_iota(jnp.int32, (pad_slots, total), 1) == target).astype(
            jnp.bfloat16
        )
        hidden[row_span(unit, 0, pad_slots), :] = jnp.dot(
            order, hidden_ref[...], preferred_element_type=jnp.float32
        ).astype(jnp.bfloat16)

    def select(unit, start, size):
        span = pl.ds(pl.multiple_of(unit * block, block), block)
        rows[0, row_span(unit, 0, pad_slots), start : start + size] = jnp.dot(
            pick[...], tokens[span, start : start + size], preferred_element_type=jnp.float32
        ).astype(jnp.bfloat16)

    def product(which, begin, end):
        span = slice(begin * pad_slots, end * pad_slots)
        return lax.dot_general(
            hidden[span, :],
            rows[which, span, :],
            (((0,), (0,)), ((), ())),
            preferred_element_type=jnp.float32,
        )

    def wait_sides(unit, parts):
        for which in parts:
            side_copy(unit, which).wait_recv()

    def settle(which, begin, end):
        for unit in range(begin, end):
            wait_sides(unit, ((), (3,), (1,), (4, 5))[which])

    def forward(unit):
        wait_sides(unit, (0, 2))
        side_copy(unit, 4).start()
        side_copy(unit, 5).start()

    def arrived(recv, place, step, index):
        if index < CHUNKS:
            a = part(place, core, index)
        else:
            a = metas.at[place * 2 + core]
        remote(a, a, next_send.at[0, index], recv.at[step, index], to_next).wait_recv()

    cut = min(feat, 512)
    early = max(0, (half - 10) // 2 + 1)

    def advance(step, carry):
        odd = lax.rem(step, 2) == 1
        unit = (step - 3) // 2
        busy = odd & (step >= 3)
        down = place_down(step)
        up = place_up(step)
        forward_next = (step < half - 1) | (core == 0)
        forward_prev = (step < half - 1) | (core == 1)
        for index in (CHUNKS, *range(CHUNKS)):
            arrived(next_recv, down, step, index)

            @pl.when(forward_next)
            def _():
                @pl.when(step >= 2)
                def _():
                    next_copy(step, index).wait_send()

                next_copy(step, index).start()

            arrived(prev_recv, up, step, index)

            @pl.when(forward_prev)
            def _():
                @pl.when(step >= 2)
                def _():
                    prev_copy(step, index).wait_send()

                prev_copy(step, index).start()

            if index == 0:

                @pl.when(busy)
                def _():
                    prepare(unit)

            if index == 1:

                @pl.when(busy)
                def _():
                    select(unit, 0, cut)

            if index == 2 and cut < feat:

                @pl.when(busy)
                def _():
                    select(unit, cut, feat - cut)

            if index == 3:

                @pl.when(busy & (unit >= 1))
                def _():
                    forward(unit - 1)

                @pl.when(busy)
                def _():
                    for which in range(4):
                        side_copy(unit, which).start()

            if early and index < CHUNKS:

                @pl.when(step == half - 2)
                def _():
                    settle(index, 0, early)
                    acc[index] = product(index, 0, early)

        @pl.when(step >= 2)
        def _():
            for copy in twin_copies(down, core, 0, step % 2):
                copy.wait_send()

        for copy in twin_copies(down, core, 0, step % 2):
            copy.start()

        @pl.when(step >= 3)
        def _():
            for copy in twin_copies(up, core, 1, step % 2):
                copy.wait_send()

        for copy in twin_copies(up, core, 1, step % 2):
            copy.start()
        return carry

    lax.fori_loop(1, half, advance, 0)

    last = place_down(half)
    for way, recv in ((0, next_recv), (1, prev_recv)):

        @pl.when(core == way)
        def _():
            for index in (CHUNKS, *range(CHUNKS)):
                arrived(recv, last, half, index)
            for copy in twin_copies(last, core, way, half % 2):
                copy.wait_send()
            for copy in twin_copies(last, core, way, half % 2):
                copy.start()

    late = max(early, units - 2)
    if late > early:
        for which in range(4):
            settle(which, early, late)
            more = product(which, early, late)
            acc[which] = acc[which] + more if early else more
    prepare(units - 1)
    select(units - 1, 0, cut)
    if cut < feat:
        select(units - 1, cut, feat - cut)
    for which in range(4):
        side_copy(units - 1, which).start()
    for unit in range(late, units):
        forward(unit)
    for which in range(4):
        settle(which, late, units)
        total = product(which, late, units)
        if late:
            total = total + acc[which]
        out_buf[which] = total.astype(out_buf.dtype)
        owner = lax.rem(side + (0, 1, sides - 1, 2)[which], sides)
        columns = pl.ds(pl.multiple_of(owner * feat, 128), feat)
        pltpu.make_async_copy(out_buf.at[which], out_ref.at[:, columns], out_sem.at[which]).start()

    for index in range(CHUNKS + 1):
        for parity in range(2):
            next_copy(half - 2 + parity, index).wait_send()
            prev_copy(half - 2 + parity, index).wait_send()
    for way in range(2):
        for parity in range(2):
            for copy in twin_copies(0, core, way, parity):
                copy.wait_send()

    def drain(unit, carry):
        for which in range(6):
            side_copy(unit, which).wait_send()
        return carry

    lax.fori_loop(0, units, drain, 0)

    @pl.when(pipe > 0)
    def _():
        for index in range(CHUNKS):
            own_remote(index).wait_send()

    for which in range(4):
        pltpu.make_async_copy(
            out_buf.at[which], out_ref.at[:, pl.ds(0, feat)], out_sem.at[which]
        ).wait()


def local(sent_grad, head_grad, probs, expert_ids, hidden_act):
    pipes = lax.axis_size("pipe")
    experts = lax.axis_size("expert")
    sides = lax.axis_size("tensor")
    chips = experts // 2
    half = chips // 2
    units = chips // 4
    tok, feat = head_grad.shape
    hid = hidden_act.shape[3]
    pad_slots = -(-8 * MOST // 16) * 16
    meta = jnp.concatenate([expert_ids[0].T.astype(jnp.bfloat16), probs[0].T], axis=0)
    bf16 = jnp.bfloat16
    dma = pltpu.SemaphoreType.DMA
    vmem = pl.BlockSpec(memory_space=pltpu.VMEM)
    anywhere = pl.BlockSpec(memory_space=pl.ANY)
    grad = pl.pallas_call(
        functools.partial(kernel, pipes, chips, sides),
        out_shape=jax.ShapeDtypeStruct((hid, sides * feat), bf16),
        in_specs=[vmem, vmem, anywhere, anywhere],
        out_specs=anywhere,
        scratch_shapes=[
            pltpu.VMEM((experts * tok, feat), bf16),
            pltpu.VMEM((experts, 2 * TOPK, tok), bf16),
            pltpu.VMEM((pad_slots, 8 * tok), bf16),
            pltpu.VMEM((units * pad_slots, hid), bf16),
            pltpu.VMEM((4, units * pad_slots, feat), bf16),
            pltpu.VMEM((4, hid, feat), jnp.float32),
            pltpu.VMEM((4, hid, feat), bf16),
            dma((CHUNKS,)),
            dma((CHUNKS,)),
            dma((2, CHUNKS + 1)),
            dma((half + 1, CHUNKS + 1)),
            dma((2, CHUNKS + 1)),
            dma((half + 1, CHUNKS + 1)),
            dma((2, 2, 2)),
            dma((chips, 2)),
            dma((units, 6)),
            dma((units, 6)),
            dma((4,)),
        ],
        compiler_params=pltpu.CompilerParams(
            collective_id=0, has_side_effects=True, vmem_limit_bytes=60_000_000
        ),
    )(meta, hidden_act[0, 0], sent_grad[0], head_grad)
    return grad[None, None]


def solution(mesh):
    in_specs = (
        P("pipe", "expert", "tensor"),
        P("expert", "tensor"),
        P("pipe", "expert", None),
        P("pipe", "expert", None),
        P("pipe", "expert", None, "tensor"),
    )
    out_specs = P("pipe", "expert", "tensor", None)
    return jax.shard_map(local, mesh=mesh, in_specs=in_specs, out_specs=out_specs, check_vma=False)
```

time: 290 us -> 133 us (0.46)
  waiting for transfers between devices: 182 us -> 0 us
  Pallas kernels: 0 us -> 128 us
  blocking collectives: 72.6 us -> 0 us
  matrix products: 13.4 us -> 0 us
  between operations: 13.4 us -> 0.01 us
    all_gather x2 -> x0, waiting for transfers between devices: 175 us -> none  [the longest x1 89.1 us: local(): tokens = lax.all_gather(incoming, 'expert', axis=0)]
    pallas_call x0 -> x1, Pallas kernels: none -> 128 us  [local(): pl.pallas_call(functools.partial(kernel, pipes, chips, sides), out_shape=...]
    all_gather x1 -> x0, blocking collectives: 72.6 us -> none  [local(): metas = lax.all_gather(meta, 'expert', axis=0)]
    dot_general x3 -> x0, matrix products: 13.4 us -> none  [the longest x1 7.47 us: local(): jnp.einsum('brn,bnd->brd', pick, tokens, preferred_element_type=jnp.float32)]
    ppermute x1 -> x0, waiting for transfers between devices: 6.34 us -> none  [local(): shifted = lax.ppermute(sent_grad, 'pipe', pairs)]
  transfers between devices with their start and end apart: 3 -> 0, of which waited for: 3 -> 0; matrix products, arithmetic and copies ran while one was open for 1% -> 0% of each run, Pallas kernels for 0% -> 0%
where the time goes in v2:
time: 133 us
  Pallas kernels  128 us (96%)
  local copies, waits for them, and re-layouts  2.85 us (2%)
  other arithmetic  1.96 us (1%)
    pallas_call x1, Pallas kernels, local(): pl.pallas_call(functools.partial(kernel, pipes, chips, sides), out_shape=...  128 us
    unnamed x1, local copies, waits for them, and re-layouts  2.85 us

profile of v2, /device:TPU:1, one launch (start us, length us, event | category | flops | bytes accessed | tf_op | source)
XLA Modules:
  0.0 132.7 jit_solution(14540454422933382951)
XLA Ops:
  0.0 0.7 convert_bitcast_fusion
  0.7 1.3 pad_maximum_fusion.meta_ref
  2.0 127.9 %shard_map.55 = bf16[256,3584]{1,0:T(8,128)(2,1)} custom-call(bf16[16,128]{1,0:T(8,128)(2,1)} %pad_maximum_fusion.meta_ref, bf16[1088,256]{1,0:T(8,128)(2,1)} %bitcast.11, bf16[128,896]{1,0:T(8,128)(2,1)} %bitcast.12, bf16[128,896]{1,0:T(8,128)(2,1)} %head_ref.1), custom_call_target="tpu_custom_call" | custom-call | tf_op jit(solution)/shard_map/pallas_call | solution.py:442
  129.9 2.8 %copy.7 = bf16[1,1,256,3584]{3,2,1,0:T(8,128)(2,1)} copy(bf16[1,1,256,3584]{3,2,1,0:T(8,128)(2,1)} %bitcast.10) | data formatting | bytes 3670016

commit v3 on v2

--- a/solution.py
+++ b/solution.py
@@ -11,20 +11,26 @@
 MOST = 17
 CHUNKS = 4
 MESH = pl.DeviceIdType.MESH
+SIDE_PARTS = ((), (3,), (1,), (4, 5))
 
 
 def kernel(
     pipes,
     chips,
     sides,
-    meta_ref,
+    ids_ref,
+    probs_ref,
     hidden_ref,
     sent_ref,
     head_ref,
     out_ref,
     tokens,
     metas,
-    pick,
+    pick_a,
+    pick_b,
+    ids_in,
+    probs_in,
+    hidden_in,
     hidden,
     rows,
     acc,
@@ -46,9 +52,8 @@
     half = chips // 2
     units = chips // 4
     block = 8 * tok
-    unit_slots = 8 * MOST
     pad_slots = rows.shape[1] // units
-    first = (pad_slots // 32) * 16 + (16 if pad_slots % 32 else 0)
+    lead = pick_a.shape[0]
     hid = hidden_ref.shape[1]
 
     me = lax.axis_index("expert")
@@ -60,8 +65,11 @@
     to_next = {"expert": lax.rem(me + 2, experts)}
     to_prev = {"expert": lax.rem(me + experts - 2, experts)}
     to_twin = {"expert": me + 1 - 2 * core}
-    to_right = {"tensor": lax.rem(side + 1, sides)}
-    to_left = {"tensor": lax.rem(side + sides - 1, sides)}
+    turn = 1 - 2 * core
+    right = lax.rem(side + sides + turn, sides)
+    left = lax.rem(side + sides - turn, sides)
+    to_right = {"tensor": right}
+    to_left = {"tensor": left}
     to_lower = {"pipe": lax.rem(pipe + pipes - 1, pipes)}
     to_upper = {"pipe": lax.rem(pipe + 1, pipes)}
 
@@ -141,9 +149,14 @@
     def row_span(unit, start, size):
         return pl.ds(pl.multiple_of(unit * pad_slots + start, 16), size)
 
-    def side_copy(unit, which):
-        a = row_span(unit, 0, first)
-        b = row_span(unit, first, pad_slots - first)
+    def side_copy(unit, kind, which):
+        if kind == 0:
+            cut_a, cut_b = (0, lead // 2), (lead // 2, lead // 2)
+        else:
+            rest = pad_slots - lead
+            size = (rest // 32) * 16 + (16 if rest % 32 else 0)
+            cut_a, cut_b = (lead, size), (lead + size, rest - size)
+        a, b = row_span(unit, *cut_a), row_span(unit, *cut_b)
         src, dst, span, device = (
             (0, 2, a, to_right),
             (0, 2, b, to_right),
@@ -155,13 +168,22 @@
         return remote(
             rows.at[src, span, :],
             rows.at[dst, span, :],
-            side_send.at[unit, which],
-            side_recv.at[unit, which],
+            side_send.at[unit, kind, which],
+            side_recv.at[unit, kind, which],
             device,
         )
 
-    own_meta = pltpu.make_async_copy(meta_ref, metas.at[core], out_sem.at[0])
-    own_meta.start()
+    own_ids = pltpu.make_async_copy(ids_ref, ids_in, out_sem.at[1])
+    own_probs = pltpu.make_async_copy(probs_ref, probs_in, out_sem.at[2])
+    own_hidden = pltpu.make_async_copy(hidden_ref, hidden_in, out_sem.at[0])
+    own_ids.start()
+    own_probs.start()
+    own_hidden.start()
+    own_ids.wait()
+    own_probs.wait()
+    metas[core] = jnp.concatenate(
+        [ids_in[...].astype(jnp.float32), probs_in[...].astype(jnp.float32)], axis=0
+    ).astype(metas.dtype)
 
     @pl.when(pipe == pipes - 1)
     def _():
@@ -178,7 +200,6 @@
         for index in range(CHUNKS):
             own_remote(index).start()
 
-    own_meta.wait()
     next_copy(0, CHUNKS).start()
     prev_copy(0, CHUNKS).start()
     for index in range(CHUNKS):
@@ -195,35 +216,42 @@
         prev_copy(0, index).start()
     for copy in twin_copies(0, core, 0, 0):
         copy.start()
-
-    slot_iota = lax.broadcasted_iota(jnp.int32, (pad_slots, tok), 0).astype(jnp.float32)
+    own_hidden.wait()
+
     before = (
         lax.broadcasted_iota(jnp.int32, (tok, tok), 0)
         < lax.broadcasted_iota(jnp.int32, (tok, tok), 1)
     ).astype(jnp.float32)
     mine = me.astype(jnp.float32)
 
-    def unit_places(unit):
-        return [4 * unit + q for q in range(4)]
-
-    def prepare(unit):
-        for place in unit_places(unit):
-            for copy in twin_copies(place, 1 - core, 0, 0):
+    def twin_wait(unit, quarters):
+        for q in quarters:
+            for copy in twin_copies(4 * unit + q, 1 - core, 0, 0):
                 copy.wait_recv()
+
+    def mark(pick, unit, blocks, base):
         gates, hits = [], []
-        for b in range(8):
+        for b in blocks:
             meta = metas[unit * 8 + b].astype(jnp.float32)
             hit = meta[:TOPK] == mine
             gates.append(jnp.sum(jnp.where(hit, meta[TOPK:], 0.0), axis=0, keepdims=True))
             hits.append(jnp.sum(jnp.where(hit, 1.0, 0.0), axis=0, keepdims=True))
-        routed = jnp.concatenate(hits, axis=0)
+        spare = jnp.zeros((8 - len(blocks), tok), jnp.float32)
+        routed = jnp.concatenate([*hits, spare], axis=0)
         rank = jnp.dot(routed, before, preferred_element_type=jnp.float32)
-        for b in range(8):
-            slot = jnp.where(routed[b : b + 1] > 0.5, rank[b : b + 1] + b * MOST, -1.0)
-            pick[:, b * tok : (b + 1) * tok] = jnp.where(
-                slot_iota == slot, gates[b], 0.0
-            ).astype(jnp.bfloat16)
-        total = hidden_ref.shape[0]
+        slots = (
+            lax.broadcasted_iota(jnp.int32, (pick.shape[0], tok), 0) + base
+        ).astype(jnp.float32)
+        for n, b in enumerate(blocks):
+            slot = jnp.where(routed[n : n + 1] > 0.5, rank[n : n + 1] + b * MOST, -1.0)
+            pick[:, n * tok : (n + 1) * tok] = jnp.where(slots == slot, gates[n], 0.0).astype(
+                pick.dtype
+            )
+
+    def prepare_a(unit):
+        twin_wait(unit, (0, 1, 2))
+        mark(pick_a, unit, range(6), 0)
+        total = hidden_in.shape[0]
         i = lax.broadcasted_iota(jnp.int32, (pad_slots, total), 0)
         width = 2 * MOST
         offsets = (2 * unit, 2 * unit + 1, chips - 2 * unit - 1, chips - 2 * unit - 2)
@@ -236,17 +264,26 @@
             jnp.bfloat16
         )
         hidden[row_span(unit, 0, pad_slots), :] = jnp.dot(
-            order, hidden_ref[...], preferred_element_type=jnp.float32
+            order, hidden_in[...], preferred_element_type=jnp.float32
         ).astype(jnp.bfloat16)
 
-    def select(unit, start, size):
-        span = pl.ds(pl.multiple_of(unit * block, block), block)
-        rows[0, row_span(unit, 0, pad_slots), start : start + size] = jnp.dot(
+    def prepare_b(unit):
+        twin_wait(unit, (3,))
+        mark(pick_b, unit, range(5, 8), lead)
+
+    def select(unit, kind, start, size):
+        pick, base, skip = ((pick_a, 0, 0), (pick_b, lead, 5 * tok))[kind]
+        span = pl.ds(pl.multiple_of(unit * block + skip, tok), pick.shape[1])
+        rows[0, row_span(unit, base, pick.shape[0]), start : start + size] = jnp.dot(
             pick[...], tokens[span, start : start + size], preferred_element_type=jnp.float32
         ).astype(jnp.bfloat16)
 
+    def send(unit, kind):
+        for which in range(4):
+            side_copy(unit, kind, which).start()
+
     def product(which, begin, end):
-        span = slice(begin * pad_slots, end * pad_slots)
+        span = slice(begin, end)
         return lax.dot_general(
             hidden[span, :],
             rows[which, span, :],
@@ -254,18 +291,19 @@
             preferred_element_type=jnp.float32,
         )
 
-    def wait_sides(unit, parts):
+    def wait_sides(unit, kind, parts):
         for which in parts:
-            side_copy(unit, which).wait_recv()
+            side_copy(unit, kind, which).wait_recv()
 
     def settle(which, begin, end):
         for unit in range(begin, end):
-            wait_sides(unit, ((), (3,), (1,), (4, 5))[which])
-
-    def forward(unit):
-        wait_sides(unit, (0, 2))
-        side_copy(unit, 4).start()
-        side_copy(unit, 5).start()
+            for kind in range(2):
+                wait_sides(unit, kind, SIDE_PARTS[which])
+
+    def forward(unit, kind):
+        wait_sides(unit, kind, (0, 2))
+        side_copy(unit, kind, 4).start()
+        side_copy(unit, kind, 5).start()
 
     def arrived(recv, place, step, index):
         if index < CHUNKS:
@@ -275,12 +313,15 @@
         remote(a, a, next_send.at[0, index], recv.at[step, index], to_next).wait_recv()
 
     cut = min(feat, 512)
-    early = max(0, (half - 10) // 2 + 1)
+    early = max(0, (half - 9) // 2 + 1)
+    wide = cut < feat
 
     def advance(step, carry):
-        odd = lax.rem(step, 2) == 1
-        unit = (step - 3) // 2
-        busy = odd & (step >= 3)
+        even = lax.rem(step, 2) == 0
+        unit_a = (step - 2) // 2
+        unit_b = (step - 3) // 2
+        busy_a = even & (step >= 2)
+        busy_b = (lax.rem(step, 2) == 1) & (step >= 3)
         down = place_down(step)
         up = place_up(step)
         forward_next = (step < half - 1) | (core == 0)
@@ -308,39 +349,43 @@
 
             if index == 0:
 
-                @pl.when(busy)
-                def _():
-                    prepare(unit)
-
-            if index == 1:
-
-                @pl.when(busy)
-                def _():
-                    select(unit, 0, cut)
-
-            if index == 2 and cut < feat:
-
-                @pl.when(busy)
-                def _():
-                    select(unit, cut, feat - cut)
-
-            if index == 3:
-
-                @pl.when(busy & (unit >= 1))
-                def _():
-                    forward(unit - 1)
-
-                @pl.when(busy)
-                def _():
-                    for which in range(4):
-                        side_copy(unit, which).start()
-
-            if early and index < CHUNKS:
+                @pl.when(busy_a & (step >= 4))
+                def _():
+                    forward(unit_a - 1, 0)
+
+                @pl.when(busy_a)
+                def _():
+                    prepare_a(unit_a)
+
+                @pl.when(busy_b & (step >= 5))
+                def _():
+                    forward(unit_b - 1, 1)
+
+                @pl.when(busy_b)
+                def _():
+                    prepare_b(unit_b)
+
+            for kind, busy, unit in ((0, busy_a, unit_a), (1, busy_b, unit_b)):
+                if index == 1:
+
+                    @pl.when(busy)
+                    def _():
+                        select(unit, kind, 0, cut)
+
+                if index == 2:
+
+                    @pl.when(busy)
+                    def _():
+                        if wide:
+                            select(unit, kind, cut, feat - cut)
+                        send(unit, kind)
+
+            if early and index < 4:
 
                 @pl.when(step == half - 2)
                 def _():
                     settle(index, 0, early)
-                    acc[index] = product(index, 0, early)
+                    acc[index] = product(index, 0, early * pad_slots)
 
         @pl.when(step >= 2)
         def _():
@@ -360,6 +405,17 @@
         return carry
 
     lax.fori_loop(1, half, advance, 0)
+
+    def finish(unit, kind):
+        (prepare_a, prepare_b)[kind](unit)
+        select(unit, kind, 0, cut)
+        if wide:
+            select(unit, kind, cut, feat - cut)
+        send(unit, kind)
+
+    if units > 1:
+        forward(units - 2, 0)
+    finish(units - 1, 0)
 
     last = place_down(half)
     for way, recv in ((0, next_recv), (1, prev_recv)):
@@ -374,26 +430,32 @@
                 copy.start()
 
     late = max(early, units - 2)
+    split = (units - 1) * pad_slots + lead
+    if units > 1:
+        forward(units - 2, 1)
     if late > early:
         for which in range(4):
             settle(which, early, late)
-            more = product(which, early, late)
+            more = product(which, early * pad_slots, late * pad_slots)
             acc[which] = acc[which] + more if early else more
-    prepare(units - 1)
-    select(units - 1, 0, cut)
-    if cut < feat:
-        select(units - 1, cut, feat - cut)
+    finish(units - 1, 1)
+
+    def gather_up(which):
+        settle(which, late, units - 1)
+        wait_sides(units - 1, 0, SIDE_PARTS[which])
+        more = product(which, late * pad_slots, split)
+        acc[which] = acc[which] + more if late else more
+
+    forward(units - 1, 0)
+    for which in range(3):
+        gather_up(which)
+    forward(units - 1, 1)
+    gather_up(3)
     for which in range(4):
-        side_copy(units - 1, which).start()
-    for unit in range(late, units):
-        forward(unit)
-    for which in range(4):
-        settle(which, late, units)
-        total = product(which, late, units)
-        if late:
-            total = total + acc[which]
+        wait_sides(units - 1, 1, SIDE_PARTS[which])
+        total = acc[which] + product(which, split, units * pad_slots)
         out_buf[which] = total.astype(out_buf.dtype)
-        owner = lax.rem(side + (0, 1, sides - 1, 2)[which], sides)
+        owner = (side, right, left, lax.rem(side + 2, sides))[which]
         columns = pl.ds(pl.multiple_of(owner * feat, 128), feat)
         pltpu.make_async_copy(out_buf.at[which], out_ref.at[:, columns], out_sem.at[which]).start()
 
@@ -407,8 +469,9 @@
                 copy.wait_send()
 
     def drain(unit, carry):
-        for which in range(6):
-            side_copy(unit, which).wait_send()
+        for kind in range(2):
+            for which in range(6):
+                side_copy(unit, kind, which).wait_send()
         return carry
 
     lax.fori_loop(0, units, drain, 0)
@@ -434,20 +497,25 @@
     tok, feat = head_grad.shape
     hid = hidden_act.shape[3]
     pad_slots = -(-8 * MOST // 16) * 16
-    meta = jnp.concatenate([expert_ids[0].T.astype(jnp.bfloat16), probs[0].T], axis=0)
+    lead = 96
     bf16 = jnp.bfloat16
     dma = pltpu.SemaphoreType.DMA
     vmem = pl.BlockSpec(memory_space=pltpu.VMEM)
     anywhere = pl.BlockSpec(memory_space=pl.ANY)
+    hbm = pl.BlockSpec(memory_space=pltpu.HBM)
     grad = pl.pallas_call(
         functools.partial(kernel, pipes, chips, sides),
         out_shape=jax.ShapeDtypeStruct((hid, sides * feat), bf16),
-        in_specs=[vmem, vmem, anywhere, anywhere],
+        in_specs=[hbm, hbm, hbm, hbm, hbm],
         out_specs=anywhere,
         scratch_shapes=[
             pltpu.VMEM((experts * tok, feat), bf16),
             pltpu.VMEM((experts, 2 * TOPK, tok), bf16),
-            pltpu.VMEM((pad_slots, 8 * tok), bf16),
+            pltpu.VMEM((lead, 6 * tok), bf16),
+            pltpu.VMEM((pad_slots - lead, 3 * tok), bf16),
+            pltpu.VMEM((TOPK, tok), jnp.int32),
+            pltpu.VMEM((TOPK, tok), bf16),
+            pltpu.VMEM(hidden_act.shape[2:], bf16),
             pltpu.VMEM((units * pad_slots, hid), bf16),
             pltpu.VMEM((4, units * pad_slots, feat), bf16),
             pltpu.VMEM((4, hid, feat), jnp.float32),
@@ -460,14 +528,14 @@
             dma((half + 1, CHUNKS + 1)),
             dma((2, 2, 2)),
             dma((chips, 2)),
-            dma((units, 6)),
-            dma((units, 6)),
+            dma((units, 2, 6)),
+            dma((units, 2, 6)),
             dma((4,)),
         ],
         compiler_params=pltpu.CompilerParams(
-            collective_id=0, has_side_effects=True, vmem_limit_bytes=60_000_000
+            collective_id=0, has_side_effects=True, vmem_limit_bytes=36_000_000
         ),
-    )(meta, hidden_act[0, 0], sent_grad[0], head_grad)
+    )(*(pltpu.with_memory_space_constraint(a, pltpu.HBM) for a in (expert_ids[0].T, probs[0].T, hidden_act[0, 0], sent_grad[0], head_grad)))
     return grad[None, None]
 
 

time: 133 us -> 122 us (0.917)
  Pallas kernels: 128 us -> 120 us
  other arithmetic: 1.96 us -> 0 us
  local copies, waits for them, and re-layouts: 2.85 us -> 1.23 us
    pallas_call x1, Pallas kernels: 128 us -> 120 us  [local(): pl.pallas_call(functools.partial(kernel, pipes, chips, sides), out_shape=...]
    unnamed x1, local copies, waits for them, and re-layouts: 2.85 us -> 1.23 us
where the time goes in v3:
time: 122 us
  Pallas kernels  120 us (98%)
  local copies, waits for them, and re-layouts  1.23 us (1%)
    pallas_call x1, Pallas kernels, local(): pl.pallas_call(functools.partial(kernel, pipes, chips, sides), out_shape=...  120 us

profile of v3, /device:TPU:1, one launch (start us, length us, event | category | flops | bytes accessed | tf_op | source)
XLA Modules:
  0.0 121.5 jit_solution(8318063879693045640)
XLA Ops:
  0.0 120.3 %shard_map.55 = bf16[256,3584]{1,0:T(8,128)(2,1)S(1)} custom-call(s32[8,128]{1,0:T(8,128)} %bitcast.12, bf16[8,128]{1,0:T(8,128)(2,1)} %bitcast.13, bf16[1088,256]{1,0:T(8,128)(2,1)} %bitcast.10, bf16[128,896]{1,0:T(8,128)(2,1)} %bitcast.11, bf16[128,896]{1,0:T(8,128)(2,1)} %head_ref.1), custom_call_target="tpu_custom_call" | custom-call | tf_op jit(solution)/shard_map/pallas_call | solution.py:506
  120.3 1.2 %copy.7 = bf16[1,1,256,3584]{3,2,1,0:T(8,128)(2,1)} copy(bf16[1,1,256,3584]{3,2,1,0:T(8,128)(2,1)S(1)} %bitcast.9) | data formatting | bytes 3670016

commit v4 on v3

--- a/solution.py
+++ b/solution.py
@@ -28,6 +28,7 @@
     metas,
     pick_a,
     pick_b,
+    pick_c,
     ids_in,
     probs_in,
     hidden_in,
@@ -53,7 +54,7 @@
     units = chips // 4
     block = 8 * tok
     pad_slots = rows.shape[1] // units
-    lead = pick_a.shape[0]
+    starts = (0, pick_a.shape[0], pick_a.shape[0] + pick_b.shape[0], pad_slots)
     hid = hidden_ref.shape[1]
 
     me = lax.axis_index("expert")
@@ -150,12 +151,9 @@
         return pl.ds(pl.multiple_of(unit * pad_slots + start, 16), size)
 
     def side_copy(unit, kind, which):
-        if kind == 0:
-            cut_a, cut_b = (0, lead // 2), (lead // 2, lead // 2)
-        else:
-            rest = pad_slots - lead
-            size = (rest // 32) * 16 + (16 if rest % 32 else 0)
-            cut_a, cut_b = (lead, size), (lead + size, rest - size)
+        size = starts[kind + 1] - starts[kind]
+        fore = -(-size // 32) * 16
+        cut_a, cut_b = (starts[kind], fore), (starts[kind] + fore, size - fore)
         a, b = row_span(unit, *cut_a), row_span(unit, *cut_b)
         src, dst, span, device = (
             (0, 2, a, to_right),
@@ -248,9 +246,7 @@
                 pick.dtype
             )
 
-    def prepare_a(unit):
-        twin_wait(unit, (0, 1, 2))
-        mark(pick_a, unit, range(6), 0)
+    def permute(unit):
         total = hidden_in.shape[0]
         i = lax.broadcasted_iota(jnp.int32, (pad_slots, total), 0)
         width = 2 * MOST
@@ -271,10 +267,17 @@
         twin_wait(unit, (3,))
         mark(pick_b, unit, range(5, 8), lead)
 
+    parts = (((0,), range(0, 2), pick_a), ((1, 2), range(1, 6), pick_b), ((3,), range(5, 8), pick_c))
+
+    def prepare(unit, kind):
+        quarters, blocks, pick = parts[kind]
+        twin_wait(unit, quarters)
+        mark(pick, unit, blocks, starts[kind])
+
     def select(unit, kind, start, size):
-        pick, base, skip = ((pick_a, 0, 0), (pick_b, lead, 5 * tok))[kind]
-        span = pl.ds(pl.multiple_of(unit * block + skip, tok), pick.shape[1])
-        rows[0, row_span(unit, base, pick.shape[0]), start : start + size] = jnp.dot(
+        pick = parts[kind][2]
+        span = pl.ds(pl.multiple_of(unit * block + parts[kind][1][0] * tok, tok), pick.shape[1])
+        rows[0, row_span(unit, starts[kind], pick.shape[0]), start : start + size] = jnp.dot(
             pick[...], tokens[span, start : start + size], preferred_element_type=jnp.float32
         ).astype(jnp.bfloat16)
 
@@ -297,7 +300,7 @@
 
     def settle(which, begin, end):
         for unit in range(begin, end):
-            for kind in range(2):
+            for kind in range(3):
                 wait_sides(unit, kind, SIDE_PARTS[which])
 
     def forward(unit, kind):
@@ -318,10 +321,11 @@
 
     def advance(step, carry):
         even = lax.rem(step, 2) == 0
-        unit_a = (step - 2) // 2
-        unit_b = (step - 3) // 2
-        busy_a = even & (step >= 2)
-        busy_b = (lax.rem(step, 2) == 1) & (step >= 3)
+        odd = lax.rem(step, 2) == 1
+        unit_a = (step - 1) // 2
+        unit_b = (step - 2) // 2
+        unit_c = (step - 3) // 2
+        work = ((odd, unit_a), (even, unit_b), (odd & (step >= 3), unit_c))
         down = place_down(step)
         up = place_up(step)
         forward_next = (step < half - 1) | (core == 0)
@@ -347,25 +351,16 @@
 
                 prev_copy(step, index).start()
 
-            if index == 0:
-
-                @pl.when(busy_a & (step >= 4))
-                def _():
-                    forward(unit_a - 1, 0)
-
-                @pl.when(busy_a)
-                def _():
-                    prepare_a(unit_a)
-
-                @pl.when(busy_b & (step >= 5))
-                def _():
-                    forward(unit_b - 1, 1)
-
-                @pl.when(busy_b)
-                def _():
-                    prepare_b(unit_b)
-
-            for kind, busy, unit in ((0, busy_a, unit_a), (1, busy_b, unit_b)):
+            for kind, (busy, unit) in enumerate(work):
+                if index == 0:
+
+                    @pl.when(busy)
+                    def _():
+                        prepare(unit, kind)
+
+                        if kind == 1:
+                            permute(unit)
+
                 if index == 1:
 
                     @pl.when(busy)
@@ -380,6 +375,20 @@
                             select(unit, kind, cut, feat - cut)
                         send(unit, kind)
 
+            if index == 3:
+
+                @pl.when(even)
+                def _():
+                    forward(unit_b, 0)
+
+                @pl.when(even & (step >= 4))
+                def _():
+                    forward(unit_b - 1, 2)
+
+                @pl.when(odd & (step >= 3))
+                def _():
+                    forward(unit_c, 1)
+
             if early and index < 4:
 
                 @pl.when(step == half - 2)
@@ -407,15 +416,13 @@
     lax.fori_loop(1, half, advance, 0)
 
     def finish(unit, kind):
-        (prepare_a, prepare_b)[kind](unit)
+        prepare(unit, kind)
         select(unit, kind, 0, cut)
         if wide:
             select(unit, kind, cut, feat - cut)
         send(unit, kind)
 
-    if units > 1:
-        forward(units - 2, 0)
-    finish(units - 1, 0)
+    finish(units - 1, 1)
 
     last = place_down(half)
     for way, recv in ((0, next_recv), (1, prev_recv)):
@@ -430,29 +437,32 @@
                 copy.start()
 
     late = max(early, units - 2)
-    split = (units - 1) * pad_slots + lead
+    split = (units - 1) * pad_slots + starts[2]
+    forward(units - 1, 0)
     if units > 1:
-        forward(units - 2, 1)
+        forward(units - 2, 2)
+    permute(units - 1)
     if late > early:
         for which in range(4):
             settle(which, early, late)
             more = product(which, early * pad_slots, late * pad_slots)
             acc[which] = acc[which] + more if early else more
-    finish(units - 1, 1)
+    finish(units - 1, 2)
 
     def gather_up(which):
         settle(which, late, units - 1)
         wait_sides(units - 1, 0, SIDE_PARTS[which])
+        wait_sides(units - 1, 1, SIDE_PARTS[which])
         more = product(which, late * pad_slots, split)
         acc[which] = acc[which] + more if late else more
 
-    forward(units - 1, 0)
+    forward(units - 1, 1)
     for which in range(3):
         gather_up(which)
-    forward(units - 1, 1)
+    forward(units - 1, 2)
     gather_up(3)
     for which in range(4):
-        wait_sides(units - 1, 1, SIDE_PARTS[which])
+        wait_sides(units - 1, 2, SIDE_PARTS[which])
         total = acc[which] + product(which, split, units * pad_slots)
         out_buf[which] = total.astype(out_buf.dtype)
         owner = (side, right, left, lax.rem(side + 2, sides))[which]
@@ -469,7 +479,7 @@
                 copy.wait_send()
 
     def drain(unit, carry):
-        for kind in range(2):
+        for kind in range(3):
             for which in range(6):
                 side_copy(unit, kind, which).wait_send()
         return carry
@@ -497,7 +507,6 @@
     tok, feat = head_grad.shape
     hid = hidden_act.shape[3]
     pad_slots = -(-8 * MOST // 16) * 16
-    lead = 96
     bf16 = jnp.bfloat16
     dma = pltpu.SemaphoreType.DMA
     vmem = pl.BlockSpec(memory_space=pltpu.VMEM)
@@ -511,8 +520,9 @@
         scratch_shapes=[
             pltpu.VMEM((experts * tok, feat), bf16),
             pltpu.VMEM((experts, 2 * TOPK, tok), bf16),
-            pltpu.VMEM((lead, 6 * tok), bf16),
-            pltpu.VMEM((pad_slots - lead, 3 * tok), bf16),
+            pltpu.VMEM((32, 2 * tok), bf16),
+            pltpu.VMEM((64, 5 * tok), bf16),
+            pltpu.VMEM((pad_slots - 96, 3 * tok), bf16),
             pltpu.VMEM((TOPK, tok), jnp.int32),
             pltpu.VMEM((TOPK, tok), bf16),
             pltpu.VMEM(hidden_act.shape[2:], bf16),
@@ -528,8 +538,8 @@
             dma((half + 1, CHUNKS + 1)),
             dma((2, 2, 2)),
             dma((chips, 2)),
-            dma((units, 2, 6)),
-            dma((units, 2, 6)),
+            dma((units, 3, 6)),
+            dma((units, 3, 6)),
             dma((4,)),
         ],
         compiler_params=pltpu.CompilerParams(

time: 122 us -> 122 us (level)
  no operation moved by 1% of the time
where the time goes in v4:
time: 122 us; the launch traced here: 121 us
  Pallas kernels  120 us (98%)
  local copies, waits for them, and re-layouts  1.23 us (1%)
    pallas_call x1, Pallas kernels, local(): pl.pallas_call(functools.partial(kernel, pipes, chips, sides), out_shape=...  120 us

profile of v4, /device:TPU:1, one launch (start us, length us, event | category | flops | bytes accessed | tf_op | source)
XLA Modules:
  0.0 121.3 jit_solution(15605169399895534190)
XLA Ops:
  0.0 120.1 %shard_map.55 = bf16[256,3584]{1,0:T(8,128)(2,1)S(1)} custom-call(s32[8,128]{1,0:T(8,128)} %bitcast.12, bf16[8,128]{1,0:T(8,128)(2,1)} %bitcast.13, bf16[1088,256]{1,0:T(8,128)(2,1)} %bitcast.10, bf16[128,896]{1,0:T(8,128)(2,1)} %bitcast.11, bf16[128,896]{1,0:T(8,128)(2,1)} %head_ref.1), custom_call_target="tpu_custom_call" | custom-call | tf_op jit(solution)/shard_map/pallas_call | solution.py:515
  120.1 1.2 %copy.7 = bf16[1,1,256,3584]{3,2,1,0:T(8,128)(2,1)} copy(bf16[1,1,256,3584]{3,2,1,0:T(8,128)(2,1)S(1)} %bitcast.9) | data formatting | bytes 3670016

commit v5 on v3

--- a/solution.py
+++ b/solution.py
@@ -251,6 +251,8 @@
     def prepare_a(unit):
         twin_wait(unit, (0, 1, 2))
         mark(pick_a, unit, range(6), 0)
+
+    def permute(unit):
         total = hidden_in.shape[0]
         i = lax.broadcasted_iota(jnp.int32, (pad_slots, total), 0)
         width = 2 * MOST
@@ -356,6 +358,7 @@
                 @pl.when(busy_a)
                 def _():
                     prepare_a(unit_a)
+                    permute(unit_a)
 
                 @pl.when(busy_b & (step >= 5))
                 def _():
@@ -433,6 +436,7 @@
     split = (units - 1) * pad_slots + lead
     if units > 1:
         forward(units - 2, 1)
+    permute(units - 1)
     if late > early:
         for which in range(4):
             settle(which, early, late)

time: 122 us -> 122 us (level)
  no operation moved by 1% of the time
where the time goes in v5:
time: 122 us; the launch traced here: 121 us
  Pallas kernels  120 us (98%)
  local copies, waits for them, and re-layouts  1.23 us (1%)
    pallas_call x1, Pallas kernels, local(): pl.pallas_call(functools.partial(kernel, pipes, chips, sides), out_shape=...  120 us

profile of v5, /device:TPU:1, one launch (start us, length us, event | category | flops | bytes accessed | tf_op | source)
XLA Modules:
  0.0 121.5 jit_solution(8216605092483606872)
XLA Ops:
  0.0 120.2 %shard_map.55 = bf16[256,3584]{1,0:T(8,128)(2,1)S(1)} custom-call(s32[8,128]{1,0:T(8,128)} %bitcast.12, bf16[8,128]{1,0:T(8,128)(2,1)} %bitcast.13, bf16[1088,256]{1,0:T(8,128)(2,1)} %bitcast.10, bf16[128,896]{1,0:T(8,128)(2,1)} %bitcast.11, bf16[128,896]{1,0:T(8,128)(2,1)} %head_ref.1), custom_call_target="tpu_custom_call" | custom-call | tf_op jit(solution)/shard_map/pallas_call | solution.py:510
  120.2 1.2 %copy.7 = bf16[1,1,256,3584]{3,2,1,0:T(8,128)(2,1)} copy(bf16[1,1,256,3584]{3,2,1,0:T(8,128)(2,1)S(1)} %bitcast.9) | data formatting | bytes 3670016
